TPU v7x, 128 devices: a whole 4x4x4 slice. The times are simulated.
128 devices in a mesh: lat: 16 (over x, y), var: 8 (over z, core).
Axes of the slice: x: 4, y: 4, z: 4, core: 2. Of those that a mesh axis runs over, the one named last changes fastest.
Arguments:
- patches: bfloat16 [96, 192, 1024], P('lat', 'var'), may hold values from -6 to 6
- norm_gain: float32 [1024], replicated, may hold values from 0.25 to 1.75
- input_proj: bfloat16 [1024, 3072], replicated, may hold values from -7 to 7
- output_proj: bfloat16 [1024, 1024], replicated, may hold values from -0.1875 to 0.1875
- level_scale: float32 [40, 1024], P('var'), may hold values from 0.1 to 1.9
- level_shift: float32 [40, 1024], P('var'), may hold values from -3 to 3
- head_weight: bfloat16 [40, 1024, 320], P('var', 'lat'), may hold values from -0.1875 to 0.1875
- targets: bfloat16 [40, 96, 192, 320], P('var', 'lat'), may hold values from -6 to 6
- level_counts: int32 [4], replicated, may hold values from 13 to 37
- tile_dataset: int32 [16, 8], P('lat'), may hold values from 0 to 3
- slot_level: int32 [40], P('var'), may hold values from 0 to 39, as said below
Outputs:
- latent: bfloat16 [96, 192, 1024], P('lat', 'var')
- grad_latent: bfloat16 [96, 192, 1024], P('lat', 'var')
- grad_head: float32 [40, 1024, 320], P('var', 'lat')
Inputs may be any that keep to these rules, and one draw needn't show every extreme that they name: `slot_level`: for each j, slots j * 5 to (j + 1) * 5 - 1 hold the levels j * 5 to (j + 1) * 5 - 1 in some order.
All inputs are finite; a program needn't handle non-finite values.
Results may differ from a plain program's by a relative error of at most 0.012.
Values may be sent and summed in bfloat16 or wider, within the bound.
A program may use at most 128 MiB of HBM per device.

v0:
```python
import math
import jax
import jax.numpy as jnp
from jax import lax
from jax.sharding import PartitionSpec as P

HEADS = 16
WH = 6
WW = 12
EPS = 1e-05


def padded(array, sides, width, wrap):
    for axis, dim in sides:
        size, length = (lax.axis_size(axis), array.shape[dim])
        up = [(i, (i + 1) % size) for i in range(size if wrap else size - 1)]
        down = [(j, i) for i, j in up]
        last = lax.slice_in_dim(array, length - width, length, axis=dim)
        initial = lax.slice_in_dim(array, 0, width, axis=dim)
        before = lax.ppermute(last, axis, up)
        after = lax.ppermute(initial, axis, down)
        array = jnp.concatenate([before, array, after], axis=dim)
    return array


def layer_norm(values, gain):
    wide = values.astype(jnp.float32)
    average = jnp.mean(wide, axis=-1, keepdims=True)
    centred = wide - average
    variance = jnp.mean(centred * centred, axis=-1, keepdims=True)
    return (centred * lax.rsqrt(variance + EPS) * gain).astype(jnp.bfloat16)


def window_attention(query_ext, keyval, row_valid, heads):
    ext_rows, ext_cols, width = query_ext.shape
    head_size = width // heads
    win_rows = ext_rows // WH
    win_cols = ext_cols // WW

    def split(values, parts):
        shaped = values.reshape(win_rows, WH, win_cols, WW, parts, heads, head_size)
        return shaped.transpose(0, 2, 1, 3, 4, 5, 6).reshape(
            win_rows * win_cols, WH * WW, parts, heads, head_size
        )

    query_win = split(query_ext, 1)[:, :, 0]
    pairs = split(keyval, 2)
    key_win = pairs[:, :, 0]
    value_win = pairs[:, :, 1]
    key_mask = jnp.broadcast_to(
        row_valid.reshape(win_rows, 1, WH, 1), (win_rows, win_cols, WH, WW)
    ).reshape(win_rows * win_cols, WH * WW)
    scores = jnp.einsum(
        "wqhd,wkhd->whqk", query_win, key_win, preferred_element_type=jnp.float32
    ) / math.sqrt(head_size)
    scores = jnp.where(key_mask[:, None, None, :], scores, -jnp.inf)
    peak = jnp.max(scores, axis=-1, keepdims=True)
    weights = jnp.exp(scores - peak)
    probs = (weights / jnp.sum(weights, axis=-1, keepdims=True)).astype(jnp.bfloat16)
    mixed = jnp.einsum("whqk,wkhd->wqhd", probs, value_win, preferred_element_type=jnp.float32)
    return (
        mixed.reshape(win_rows, win_cols, WH, WW, width)
        .transpose(0, 2, 1, 3, 4)
        .reshape(ext_rows, ext_cols, width)
    )


def slot_terms(piece, target_rows, live_cols, level_scale, level_shift, heads_full):
    piece_wide = piece.astype(jnp.float32)
    rows = (
        piece_wide[None] * level_scale[:, None, None, :] + level_shift[:, None, None, :]
    ).astype(jnp.bfloat16)
    predicted = jnp.einsum("krnd,kdo->krno", rows, heads_full, preferred_element_type=jnp.float32)
    errors = ((predicted - target_rows.astype(jnp.float32)) * live_cols[:, None, :, None]).astype(
        jnp.bfloat16
    )
    back_grad = jnp.einsum("krno,kdo->krnd", errors, heads_full, preferred_element_type=jnp.float32)
    piece_grad = jnp.sum(back_grad * level_scale[:, None, None, :], axis=0)
    head_add = jnp.einsum("krnd,krno->dko", rows, errors, preferred_element_type=jnp.float32)
    return (piece_grad, head_add)


def local(
    patches,
    norm_gain,
    input_proj,
    output_proj,
    level_scale,
    level_shift,
    head_weight,
    targets,
    level_counts,
    tile_dataset,
    slot_level,
):
    band_rows, band_cols, width = patches.shape
    half_rows = WH // 2
    half_cols = WW // 2
    lat_count = lax.axis_size("lat")
    var_count = lax.axis_size("var")
    lat_place = lax.axis_index("lat")
    ext_rows = band_rows + WH
    ext_cols = band_cols + WW
    extended = padded(patches, (("lat", 0),), half_rows, False)
    extended = padded(extended, (("var", 1),), half_cols, True)
    normed_ext = layer_norm(extended, norm_gain)
    keyval = jnp.dot(
        normed_ext.reshape(-1, width), input_proj[:, width:], preferred_element_type=jnp.float32
    )
    keyval = keyval.astype(jnp.bfloat16).reshape(ext_rows, ext_cols, 2 * width)
    normed = normed_ext[half_rows : half_rows + band_rows, half_cols : half_cols + band_cols]
    queries = jnp.dot(
        normed.reshape(-1, width), input_proj[:, :width], preferred_element_type=jnp.float32
    )
    queries = queries.astype(jnp.bfloat16).reshape(band_rows, band_cols, width)
    query_ext = jnp.pad(queries, ((half_rows, WH - half_rows), (half_cols, WW - half_cols), (0, 0)))
    global_row = lat_place * band_rows - half_rows + jnp.arange(ext_rows, dtype=jnp.int32)
    row_valid = (global_row >= 0) & (global_row < lat_count * band_rows)
    mixed = window_attention(query_ext, keyval, row_valid, HEADS)
    attn = mixed[half_rows : half_rows + band_rows, half_cols : half_cols + band_cols].astype(
        jnp.bfloat16
    )
    update = jnp.dot(
        attn.reshape(-1, width), output_proj, preferred_element_type=jnp.float32
    ).reshape(band_rows, band_cols, width)
    latent = (patches.astype(jnp.float32) + update).astype(jnp.bfloat16)
    dataset_row = tile_dataset[0]
    dataset_ids = jnp.arange(level_counts.shape[0], dtype=jnp.int32)
    tile_levels = jnp.sum(
        jnp.where(dataset_row[:, None] == dataset_ids[None, :], level_counts[None, :], 0), axis=1
    )
    live_tiles = (slot_level[None, :] < tile_levels[:, None]).astype(jnp.float32)
    heads_full = lax.all_gather(head_weight, "lat", axis=1, tiled=True)
    tile_ids = jnp.arange(var_count, dtype=jnp.int32)
    piece = lax.all_gather(latent, "var", axis=1, tiled=True)
    piece_cols = piece.shape[1]
    column_tile = jnp.arange(piece_cols, dtype=jnp.int32) // band_cols
    onehot = (column_tile[:, None] == tile_ids[None, :]).astype(jnp.float32)
    column_live = jnp.dot(onehot, live_tiles)
    piece_grad, head_add = slot_terms(
        piece, targets, column_live.T, level_scale, level_shift, heads_full
    )
    latent_terms = piece_grad
    latent_terms, head_terms = (latent_terms, head_add)
    grad_latent = lax.psum_scatter(
        latent_terms.astype(jnp.bfloat16), "var", scatter_dimension=1, tiled=True
    )
    head_terms = head_terms * (1.0 / math.sqrt(lat_count * band_rows * var_count * band_cols))
    share_rows = width // lat_count
    summed = lax.psum(head_terms.astype(jnp.bfloat16), "lat").astype(jnp.float32)
    mine = lax.dynamic_slice_in_dim(summed, lat_place * share_rows, share_rows, 0)
    grad_head = jnp.transpose(mine, (1, 0, 2))
    return (latent, grad_latent, grad_head)


def solution(mesh):
    in_specs = (
        P("lat", "var", None),
        P(),
        P(),
        P(),
        P("var", None),
        P("var", None),
        P("var", "lat", None),
        P("var", "lat", None, None),
        P(),
        P("lat", None),
        P("var"),
    )
    out_specs = (P("lat", "var", None), P("lat", "var", None), P("var", "lat", None))
    return jax.shard_map(local, mesh=mesh, in_specs=in_specs, out_specs=out_specs, check_vma=False)
```

profile of v0, /device:TPU:0, one launch (start us, length us, event | category | flops | bytes accessed | tf_op | source)
XLA Modules:
  0.0 327.8 jit_solution(17000856274102400193)
XLA Ops:
  7.2 1.1 fusion.61
  8.4 3.6 %collective-permute-start = (bf16[3,24,1024]{2,1,0:T(8,128)(2,1)S(1)}, bf16[3,24,1024]{2,1,0:T(8,128)(2,1)S(1)}, u32[]{:S(2)}, u32[]{:S(2)}) collective-permute-start(bf16[3,24,1024]{2,1,0:T(8,128)(2,1)S(1)} %get-tuple-element.25), channel_id=1, source_target_pairs={{0,8},{8,16},{16,24},{24,32},{32,40},{40,48},{48,56},{56,64},{64,7... | collective-permute-start | bytes 442376 | tf_op jit(solution)/shard_map/ppermute | solution.py:20
  12.0 1.3 collective-permute-start.1
  13.3 1.8 collective-permute-done
  15.0 1.0 constant_dynamic-update-slice_fusion.1
  16.0 3.1 collective-permute-done.1
  19.3 2.9 collective-permute-start.3
  22.3 0.1 broadcast_in_dim.29
  22.4 3.2 collective-permute-done.2
  25.6 0.4 fusion.58
  26.1 1.9 multiply_reduce_fusion.1
  28.1 1.6 maximum_convert_fusion
  29.8 2.6 reshape.102
  32.4 1.3 fusion.50
  33.7 2.1 fusion.40
  35.8 0.2 pad.4
  35.9 2.1 reshape.99
  38.0 3.2 copy.47
  41.2 5.5 %fusion.15 = bf16[432,2048]{1,0:T(8,128)(2,1)} fusion(bf16[1024,3072]{1,0:T(8,128)(2,1)} %param.13, f32[432,1024]{1,0:T(8,128)S(1)} %copy-done.3, f32[1024]{0:T(1024)S(1)} %copy-done.5, f32[432]{0:T(512)S(1)} %rsqrt.13, f32[432]{0:T(512)S(1)} %div.33), kind=kOutput, calls=%fused_computation.22 | convolution fusion | flops 1814593536 | bytes 7740800 | tf_op jit(solution)/shard_map/dot_general | solution.py:107
  46.8 6.4 %reshape_reshape.3 = bf16[2,6,3,12,2,16,64]{6,5,4,3,2,1,0:T(8,128)(2,1)} reshape(bf16[432,2048]{1,0:T(8,128)(2,1)} %fusion.15) | data formatting | bytes 3538944 | tf_op jit(solution)/shard_map/reshape;reshape | solution.py:41
  53.1 2.6 copy.45
  55.8 2.7 fusion.59
  58.4 4.0 %copy.59 = bf16[6,72,1,16,64]{1,4,3,0,2:T(8,128)(2,1)} copy(bf16[6,72,1,16,64]{4,3,2,1,0:T(8,128)(2,1)} %get-tuple-element.18) | data formatting | bytes 1769472
  62.5 4.0 %copy.60 = bf16[6,72,1,16,64]{1,4,3,0,2:T(8,128)(2,1)} copy(bf16[6,72,1,16,64]{4,3,2,1,0:T(8,128)(2,1)} %get-tuple-element.19) | data formatting | bytes 1769472
  66.5 3.1 fusion.25
  69.6 1.8 fusion.62
  71.4 1.9 fusion.34
  73.3 4.0 %copy.51 = bf16[6,72,16,64]{3,2,1,0:T(8,128)(2,1)} copy(bf16[6,72,16,64]{1,3,2,0:T(8,128)(2,1)} %fusion.34) | data formatting | bytes 1769472 | tf_op jit(solution)/shard_map/whqk,wkhd->wqhd/transpose | solution.py:60
  77.3 3.9 %reshape.100 = bf16[2,3,6,12,1024]{4,3,2,1,0:T(8,128)(2,1)} reshape(bf16[6,72,16,64]{3,2,1,0:T(8,128)(2,1)} %copy.51) | data formatting | bytes 1769472 | tf_op jit(solution)/shard_map/reshape | solution.py:62
  81.2 1.4 copy.52
  82.6 1.0 reshape.101
  83.7 2.3 fusion.43
  86.0 0.7 all-gather.5.cloned.1.call-update
  86.9 0.2 fusion.52
  87.1 28.4 %all-gather.3.cloned.1.call-done = bf16[6,192,1024]{2,1,0:T(8,128)(2,1)} async-done(((bf16[6,24,1024]{2,1,0:T(8,128)(2,1)}), bf16[6,192,1024]{2,1,0:T(8,128)(2,1)}) %all-gather.3.cloned.1.call-update) | async-done | bytes 2359312 | tf_op jit(solution)/shard_map/all_gather | solution.py:135
  115.6 4.4 %convert_element_type.69 = f32[6,192,1024]{2,1,0:T(8,128)} convert(bf16[6,192,1024]{2,1,0:T(8,128)(2,1)} %all-gather.3.cloned.1.call-done) | non-fusion elementwise | flops 1179648 | bytes 7077888 | tf_op jit(solution)/shard_map/convert_element_type | solution.py:69
  119.9 48.6 %all-gather.5.cloned.1.call-done = bf16[5,1024,320]{2,1,0:T(8,128)(2,1)} async-done(((bf16[5,64,320]{2,1,0:T(8,128)(2,1)}), bf16[5,1024,320]{2,1,0:T(8,128)(2,1)}) %all-gather.5.cloned.1.call-update) | async-done | bytes 3276816 | tf_op jit(solution)/shard_map/all_gather | solution.py:133
  168.5 10.1 %multiply_convert_fusion = bf16[5,6,192,320]{3,2,1,0:T(8,128)(2,1)S(1)} fusion(bf16[5,6,192,320]{3,2,1,0:T(8,128)(2,1)} %param.18, f32[5,192]{1,0:T(8,128)S(1)} %fusion.52, bf16[5,1024,320]{2,1,0:T(8,128)(2,1)} %all-gather.5.cloned.1.call-done, f32[5,1024]{1,0:T(8,128)S(1)} %copy-done.6, f32[5,1024]{1,0:T(8,128)S(1)} %copy-done.7, ...), kind=kOutput, calls=%fused_computation.11 | convolution fusion | flops 3799941120 | bytes 15412992 | tf_op jit(solution)/shard_map/krnd,kdo->krno/dot_general | solution.py:73
  178.6 2.1 copy-done.11
  180.8 6.6 %fusion.14 = bf16[1024,5,320]{0,2,1:T(8,128)(2,1)} fusion(bf16[5,6,192,320]{3,2,1,0:T(8,128)(2,1)S(1)} %multiply_convert_fusion, f32[5,1024]{1,0:T(8,128)S(1)} %copy-done.6, f32[5,1024]{1,0:T(8,128)S(1)} %copy-done.7, f32[6,192,1024]{2,1,0:T(8,128)S(1)} %copy-done.2), kind=kOutput, calls=%fused_computation.21 | convolution fusion | flops 3795845120 | bytes 11722752 | tf_op jit(solution)/shard_map/krnd,krno->dko/dot_general | solution.py:79
  187.5 9.9 %multiply_reduce_fusion = bf16[6,192,1024]{2,1,0:T(8,128)(2,1)S(1)} fusion(f32[5,1024]{1,0:T(8,128)S(1)} %copy-done.7, bf16[5,6,192,320]{3,2,1,0:T(8,128)(2,1)} %copy-done.11, bf16[5,1024,320]{2,1,0:T(8,128)(2,1)} %all-gather.5.cloned.1.call-done), kind=kOutput, calls=%fused_computation.1 | convolution fusion | flops 3785490432 | bytes 9342976 | tf_op jit(solution)/shard_map/krno,kdo->krnd/dot_general | solution.py:77
  197.4 1.7 copy.61
  199.1 84.3 %all-reduce.3.cloned.1.call-done = bf16[1024,5,320]{0,2,1:T(8,128)(2,1)} async-done(((bf16[1024,5,320]{0,2,1:T(8,128)(2,1)}), bf16[1024,5,320]{0,2,1:T(8,128)(2,1)}) %all-reduce.3.cloned.1.call-update) | async-done | bytes 3276816 | tf_op jit(solution)/shard_map/psum | solution.py:150
  283.3 1.2 convert_bitcast_fusion
  284.5 1.1 copy.53
  285.6 33.4 %reduce-scatter.4.cloned.1.call-done = bf16[24,6144]{1,0:T(8,128)(2,1)} async-done(((bf16[192,6144]{1,0:T(8,128)(2,1)}), bf16[24,6144]{1,0:T(8,128)(2,1)}) %reduce-scatter.4.cloned.1.call-update) | async-done | bytes 294928
  319.1 1.3 reshape.107
  320.4 0.9 copy.58
  (44 shorter events, 0.8 us)
Async XLA Ops:
  7.2 76.5 %copy-start = (bf16[1024,1024]{1,0:T(8,128)(2,1)S(1)}, bf16[1024,1024]{1,0:T(8,128)(2,1)}, u32[]{:S(2)}) copy-start(bf16[1024,1024]{1,0:T(8,128)(2,1)} %param.14) | copy-start | bytes 6291460
  7.2 108.4 %all-gather.3.cloned.1.call-start = ((), (), s32[]{:S(2)}) async-start(), calls=%async_computation.1 | async-start | bytes 2654208 | tf_op jit(solution)/shard_map/all_gather | solution.py:135
  8.4 6.7 %collective-permute-start = (bf16[3,24,1024]{2,1,0:T(8,128)(2,1)S(1)}, bf16[3,24,1024]{2,1,0:T(8,128)(2,1)S(1)}, u32[]{:S(2)}, u32[]{:S(2)}) collective-permute-start(bf16[3,24,1024]{2,1,0:T(8,128)(2,1)S(1)} %get-tuple-element.25), channel_id=1, source_target_pairs={{0,8},{8,16},{16,24},{24,32},{32,40},{40,48},{48,56},{56,64},{64,7... | collective-permute-start | bytes 442376 | tf_op jit(solution)/shard_map/ppermute | solution.py:20
  12.0 7.2 %collective-permute-start.1 = (bf16[3,24,1024]{2,1,0:T(8,128)(2,1)S(1)}, bf16[3,24,1024]{2,1,0:T(8,128)(2,1)S(1)}, u32[]{:S(2)}, u32[]{:S(2)}) collective-permute-start(bf16[3,24,1024]{2,1,0:T(8,128)(2,1)S(1)} %get-tuple-element.24), channel_id=1, source_target_pairs={{8,0},{16,8},{24,16},{32,24},{40,32},{48,40},{56,48},{64,56},{72,6... | collective-permute-start | bytes 442376 | tf_op jit(solution)/shard_map/ppermute | solution.py:21
  19.2 6.3 %collective-permute-start.2 = (bf16[12,6,1024]{2,1,0:T(8,128)(2,1)S(1)}, bf16[12,6,1024]{2,1,0:T(8,128)(2,1)S(1)}, u32[]{:S(2)}, u32[]{:S(2)}) collective-permute-start(bf16[12,6,1024]{2,1,0:T(8,128)(2,1)S(1)} %get-tuple-element.22), channel_id=1, source_target_pairs={{0,1},{1,2},{2,3},{3,4},{4,5},{5,6},{6,7},{7,0},{8,9},{9,10},{10,1... | collective-permute-start | bytes 442376 | tf_op jit(solution)/shard_map/ppermute | solution.py:20
  19.3 6.3 %collective-permute-start.3 = (bf16[12,6,1024]{2,1,0:T(8,128)(2,1)S(1)}, bf16[12,6,1024]{2,1,0:T(8,128)(2,1)S(1)}, u32[]{:S(2)}, u32[]{:S(2)}) collective-permute-start(bf16[12,6,1024]{2,1,0:T(8,128)(2,1)S(1)} %get-tuple-element.23), channel_id=1, source_target_pairs={{1,0},{2,1},{3,2},{4,3},{5,4},{6,5},{7,6},{0,7},{9,8},{10,9},{11,1... | collective-permute-start | bytes 442376 | tf_op jit(solution)/shard_map/ppermute | solution.py:21
  27.9 4.4 %copy-start.5 = (f32[1024]{0:T(1024)S(1)}, f32[1024]{0:T(1024)}, u32[]{:S(2)}) copy-start(f32[1024]{0:T(1024)} %param.12) | copy-start | bytes 12292
  38.0 3.2 copy-start.3
  69.6 1.8 copy-start.4
  82.6 4.2 %copy-start.8 = (s32[4]{0:T(128)S(1)}, s32[4]{0:T(128)}, u32[]{:S(2)}) copy-start(s32[4]{0:T(128)} %param.19) | copy-start | bytes 52
  82.6 4.2 %copy-start.9 = (s32[1,8]{1,0:T(1,128)S(1)}, s32[1,8]{1,0:T(1,128)}, u32[]{:S(2)}) copy-start(s32[1,8]{1,0:T(1,128)} %param.20) | copy-start | bytes 100
  82.6 4.3 %copy-start.10 = (s32[5]{0:T(128)S(1)}, s32[5]{0:T(128)}, u32[]{:S(2)}) copy-start(s32[5]{0:T(128)} %param.21) | copy-start | bytes 64
  86.0 82.5 %all-gather.5.cloned.1.call-start = ((), (), s32[]{:S(2)}) async-start(), calls=%async_computation.2 | async-start | bytes 4177920 | tf_op jit(solution)/shard_map/all_gather | solution.py:133
  86.7 196.6 %all-reduce.3.cloned.1.call-start = ((), (), s32[]{:S(2)}) async-start(), calls=%async_computation.3 | async-start | bytes 6553600 | tf_op jit(solution)/shard_map/psum | solution.py:150
  87.1 81.4 %copy-start.6 = (f32[5,1024]{1,0:T(8,128)S(1)}, f32[5,1024]{1,0:T(8,128)}, u32[]{:S(2)}) copy-start(f32[5,1024]{1,0:T(8,128)} %param.16) | copy-start | bytes 61444
  87.1 81.4 %copy-start.7 = (f32[5,1024]{1,0:T(8,128)S(1)}, f32[5,1024]{1,0:T(8,128)}, u32[]{:S(2)}) copy-start(f32[5,1024]{1,0:T(8,128)} %param.15) | copy-start | bytes 61444
  168.5 12.3 %copy-start.2 = (f32[6,192,1024]{2,1,0:T(8,128)S(1)}, f32[6,192,1024]{2,1,0:T(8,128)}, u32[]{:S(2)}) copy-start(f32[6,192,1024]{2,1,0:T(8,128)} %convert_element_type.69) | copy-start | bytes 14155780
  178.6 2.2 copy-start.11
  187.4 131.6 %reduce-scatter.4.cloned.1.call-start = ((), (), s32[]{:S(2)}) async-start(), calls=%async_computation.4 | async-start | bytes 2654208
  197.4 123.9 %copy-start.1 = (bf16[1024,1024]{1,0:T(8,128)(2,1)S(1)}, bf16[1024,1024]{1,0:T(8,128)(2,1)}, u32[]{:S(2)}) copy-start(bf16[1024,1024]{1,0:T(8,128)(2,1)} %param.14) | copy-start | bytes 6291460
Sparse Core Ops, SparseCore 0:
  86.1 29.4 all-gather.2
  117.7 50.7 all-gather.4
  187.6 95.7 all-reduce.2
  285.8 33.2 reduce-scatter.3
where the time goes:
time: 329 us; the launch traced here: 328 us
  waiting for transfers between devices  204 us (62%)
  local copies, waits for them, and re-layouts  48 us (15%)
  matrix products  41.6 us (13%)
  between operations  14 us (4%)
  other arithmetic  12.7 us (4%)
  starting transfers between devices  7.98 us (2%)
    psum x1, waiting for transfers between devices, local(): lax.psum(head_terms.astype(jnp.bfloat16), 'lat').astype(jnp.float32)  84.3 us
    all_gather x1, waiting for transfers between devices, local(): heads_full = lax.all_gather(head_weight, 'lat', axis=1, tiled=True)  48.6 us
    unnamed x5, waiting for transfers between devices  34.2 us
    all_gather x1, waiting for transfers between devices, local(): piece = lax.all_gather(latent, 'var', axis=1, tiled=True)  28.4 us
    unnamed x32, local copies, waits for them, and re-layouts  16.3 us
    dot_general x1, matrix products, slot_terms(): jnp.einsum('krnd,kdo->krno', rows, heads_full, preferred_element_type=jnp...  10.1 us
    dot_general x1, matrix products, slot_terms(): jnp.einsum('krno,kdo->krnd', errors, heads_full, preferred_element_type=j...  9.86 us
    another operation x2, local copies, waits for them, and re-layouts, split(): shaped = values.reshape(win_rows, WH, win_cols, WW, parts, heads, head_size)  8.98 us
  transfers between devices with their start and end apart: 8, of which 7 were waited for; matrix products, arithmetic and copies ran while one was open for 6% of the time, Pallas kernels for 0%

commit v1 on v0

--- a/solution.py
+++ b/solution.py
@@ -147,7 +147,9 @@
     )
     head_terms = head_terms * (1.0 / math.sqrt(lat_count * band_rows * var_count * band_cols))
     share_rows = width // lat_count
-    summed = lax.psum(head_terms.astype(jnp.bfloat16), "lat").astype(jnp.float32)
+    summed = jnp.sum(lax.all_gather(head_terms.astype(jnp.bfloat16), "lat"), axis=0).astype(
+        jnp.float32
+    )
     mine = lax.dynamic_slice_in_dim(summed, lat_place * share_rows, share_rows, 0)
     grad_head = jnp.transpose(mine, (1, 0, 2))
     return (latent, grad_latent, grad_head)

time: 329 us -> 599 us (1.82)
  waiting for transfers between devices: 204 us -> 402 us
  local copies, waits for them, and re-layouts: 48 us -> 92.2 us
  other arithmetic: 12.7 us -> 38.3 us
    all_gather x0 -> x1, waiting for transfers between devices: none -> 292 us  [local(): lax.all_gather(head_terms.astype(jnp.bfloat16), 'lat')]
    psum x1 -> x0, waiting for transfers between devices: 84.3 us -> none  [local(): lax.psum(head_terms.astype(jnp.bfloat16), 'lat').astype(jnp.float32)]
    unnamed x32 -> x33, local copies, waits for them, and re-layouts: 16.3 us -> 60.5 us
    reduce_sum x0 -> x1, other arithmetic: none -> 25.7 us  [local(): jnp.sum(lax.all_gather(head_terms.astype(jnp.bfloat16), 'lat'), axis=0)]
    unnamed x5, waiting for transfers between devices: 34.2 us -> 25.2 us
  transfers between devices with their start and end apart: 8 -> 8, of which waited for: 7 -> 7; matrix products, arithmetic and copies ran while one was open for 6% -> 3% of each run, Pallas kernels for 0% -> 0%
where the time goes in v1:
time: 599 us; the launch traced here: 597 us
  waiting for transfers between devices  402 us (67%)
  local copies, waits for them, and re-layouts  92.2 us (15%)
  matrix products  42.4 us (7%)
  other arithmetic  38.3 us (6%)
  between operations  14 us (2%)
  starting transfers between devices  7.98 us (1%)
    all_gather x1, waiting for transfers between devices, local(): lax.all_gather(head_terms.astype(jnp.bfloat16), 'lat')  292 us
    unnamed x33, local copies, waits for them, and re-layouts  60.5 us
    all_gather x1, waiting for transfers between devices, local(): heads_full = lax.all_gather(head_weight, 'lat', axis=1, tiled=True)  48.6 us
    all_gather x1, waiting for transfers between devices, local(): piece = lax.all_gather(latent, 'var', axis=1, tiled=True)  28.5 us
    reduce_sum x1, other arithmetic, local(): jnp.sum(lax.all_gather(head_terms.astype(jnp.bfloat16), 'lat'), axis=0)  25.7 us
    unnamed x5, waiting for transfers between devices  25.2 us
  transfers between devices with their start and end apart: 8, of which 7 were waited for; matrix products, arithmetic and copies ran while one was open for 3% of the time, Pallas kernels for 0%

profile of v1, /device:TPU:0, one launch (start us, length us, event | category | flops | bytes accessed | tf_op | source)
XLA Modules:
  0.0 597.2 jit_solution(8553723346254270200)
XLA Ops:
  7.2 1.1 fusion.61
  8.4 3.6 collective-permute-start
  12.0 1.3 collective-permute-start.1
  13.3 1.8 collective-permute-done
  15.0 1.0 constant_dynamic-update-slice_fusion.1
  16.0 3.1 collective-permute-done.1
  19.3 2.9 collective-permute-start.3
  22.4 3.2 collective-permute-done.2
  25.6 0.4 fusion.58
  26.1 1.8 multiply_reduce_fusion.1
  28.1 1.6 maximum_convert_fusion
  29.7 2.7 reshape.102
  32.4 1.3 fusion.50
  33.7 2.1 fusion.40
  35.8 0.2 pad.4
  35.9 2.1 reshape.99
  38.0 3.2 copy.44
  41.2 5.5 fusion.15
  46.8 6.4 %reshape_reshape.3 = bf16[2,6,3,12,2,16,64]{6,5,4,3,2,1,0:T(8,128)(2,1)} reshape(bf16[432,2048]{1,0:T(8,128)(2,1)} %fusion.15) | data formatting | bytes 3538944 | tf_op jit(solution)/shard_map/reshape;reshape | solution.py:41
  53.1 2.6 copy.42
  55.7 2.6 fusion.59
  58.3 4.0 copy.56
  62.4 4.0 copy.57
  66.4 3.1 fusion.25
  69.5 1.8 fusion.62
  71.3 1.9 fusion.34
  73.2 4.0 copy.48
  77.2 3.9 reshape.100
  81.1 1.4 copy.49
  82.5 1.0 reshape.101
  83.6 2.3 fusion.43
  85.9 0.7 all-gather.7.cloned.1.call-update
  86.8 0.2 fusion.52
  87.1 28.5 %all-gather.5.cloned.1.call-done = bf16[6,192,1024]{2,1,0:T(8,128)(2,1)} async-done(((bf16[6,24,1024]{2,1,0:T(8,128)(2,1)}), bf16[6,192,1024]{2,1,0:T(8,128)(2,1)}) %all-gather.5.cloned.1.call-update) | async-done | bytes 2359312 | tf_op jit(solution)/shard_map/all_gather | solution.py:135
  115.6 4.3 convert_element_type.71
  119.9 48.6 %all-gather.7.cloned.1.call-done = bf16[5,1024,320]{2,1,0:T(8,128)(2,1)} async-done(((bf16[5,64,320]{2,1,0:T(8,128)(2,1)}), bf16[5,1024,320]{2,1,0:T(8,128)(2,1)}) %all-gather.7.cloned.1.call-update) | async-done | bytes 3276816 | tf_op jit(solution)/shard_map/all_gather | solution.py:133
  168.5 10.6 %multiply_convert_fusion = bf16[5,6,192,320]{3,2,1,0:T(8,128)(2,1)S(1)} fusion(bf16[5,6,192,320]{3,2,1,0:T(8,128)(2,1)} %param.18, f32[5,192]{1,0:T(8,128)S(1)} %fusion.52, bf16[5,1024,320]{2,1,0:T(8,128)(2,1)} %all-gather.7.cloned.1.call-done, f32[5,1024]{1,0:T(8,128)S(1)} %copy-done.7, f32[5,1024]{1,0:T(8,128)S(1)} %copy-done.6, ...), kind=kOutput, calls=%fused_computation.11 | convolution fusion | flops 3799941120 | bytes 15412992 | tf_op jit(solution)/shard_map/krnd,kdo->krno/dot_general | solution.py:73
  179.2 7.2 %multiply_reduce_fusion = bf16[6,192,1024]{2,1,0:T(8,128)(2,1)S(1)} fusion(f32[5,1024]{1,0:T(8,128)S(1)} %copy-done.6, bf16[5,6,192,320]{3,2,1,0:T(8,128)(2,1)S(1)} %multiply_convert_fusion, bf16[5,1024,320]{2,1,0:T(8,128)(2,1)S(1)} %copy-done.5), kind=kOutput, calls=%fused_computation.1 | convolution fusion | flops 3785490432 | bytes 9342976 | tf_op jit(solution)/shard_map/krno,kdo->krnd/dot_general | solution.py:77
  186.4 1.6 copy.58
  188.1 9.5 %fusion.14 = bf16[1024,5,320]{0,2,1:T(8,128)(2,1)} fusion(bf16[5,6,192,320]{3,2,1,0:T(8,128)(2,1)} %copy-done.11, f32[5,1024]{1,0:T(8,128)S(1)} %copy-done.7, f32[5,1024]{1,0:T(8,128)S(1)} %copy-done.6, f32[6,192,1024]{2,1,0:T(8,128)} %convert_element_type.71), kind=kOutput, calls=%fused_computation.21 | convolution fusion | flops 3795845120 | bytes 11722752 | tf_op jit(solution)/shard_map/krnd,krno->dko/dot_general | solution.py:79
  197.6 24.5 %reduce-scatter.4.cloned.1.call-done = bf16[24,6144]{1,0:T(8,128)(2,1)} async-done(((bf16[192,6144]{1,0:T(8,128)(2,1)}), bf16[24,6144]{1,0:T(8,128)(2,1)}) %reduce-scatter.4.cloned.1.call-update) | async-done | bytes 294928
  222.1 1.3 reshape.108
  223.4 0.9 copy.55
  224.3 292.0 %all-gather.9.cloned.1.call-done = bf16[16384,5,320]{0,2,1:T(8,128)(2,1)} async-done(((bf16[1024,5,320]{0,2,1:T(8,128)(2,1)}), bf16[16384,5,320]{0,2,1:T(8,128)(2,1)}) %all-gather.9.cloned.1.call-update) | async-done | bytes 52428816 | tf_op jit(solution)/shard_map/all_gather | solution.py:150
  516.3 46.4 %copy.59 = bf16[200,8,16,1024]{3,2,1,0:T(8,128)(2,1)} copy(bf16[200,8,16,1024]{3,1,2,0:T(8,128)(2,1)} %bitcast.63) | data formatting | bytes 104857600
  562.7 25.7 %reduce_sum.62 = bf16[1024,5,320]{0,2,1:T(8,128)(2,1)} reduce(bf16[16,1024,5,320]{1,0,3,2:T(8,128)(2,1)} %bitcast.62, bf16[]{:T(256)} %constant.42.clone.1), dimensions={0}, to_apply=%region_7.8 | reduce | flops 24576000 | bytes 55705600 | tf_op jit(solution)/shard_map/reduce_sum | solution.py:150
  588.4 1.2 convert_bitcast_fusion
  589.6 1.1 copy.50
  (46 shorter events, 0.9 us)
Async XLA Ops:
  7.2 76.4 %copy-start = (bf16[1024,1024]{1,0:T(8,128)(2,1)S(1)}, bf16[1024,1024]{1,0:T(8,128)(2,1)}, u32[]{:S(2)}) copy-start(bf16[1024,1024]{1,0:T(8,128)(2,1)} %param.14) | copy-start | bytes 6291460
  7.2 108.4 %all-gather.5.cloned.1.call-start = ((), (), s32[]{:S(2)}) async-start(), calls=%async_computation.1 | async-start | bytes 2654208 | tf_op jit(solution)/shard_map/all_gather | solution.py:135
  8.4 6.7 %collective-permute-start = (bf16[3,24,1024]{2,1,0:T(8,128)(2,1)S(1)}, bf16[3,24,1024]{2,1,0:T(8,128)(2,1)S(1)}, u32[]{:S(2)}, u32[]{:S(2)}) collective-permute-start(bf16[3,24,1024]{2,1,0:T(8,128)(2,1)S(1)} %get-tuple-element.16), channel_id=1, source_target_pairs={{0,8},{8,16},{16,24},{24,32},{32,40},{40,48},{48,56},{56,64},{64,7... | collective-permute-start | bytes 442376 | tf_op jit(solution)/shard_map/ppermute | solution.py:20
  12.0 7.2 %collective-permute-start.1 = (bf16[3,24,1024]{2,1,0:T(8,128)(2,1)S(1)}, bf16[3,24,1024]{2,1,0:T(8,128)(2,1)S(1)}, u32[]{:S(2)}, u32[]{:S(2)}) collective-permute-start(bf16[3,24,1024]{2,1,0:T(8,128)(2,1)S(1)} %get-tuple-element.15), channel_id=1, source_target_pairs={{8,0},{16,8},{24,16},{32,24},{40,32},{48,40},{56,48},{64,56},{72,6... | collective-permute-start | bytes 442376 | tf_op jit(solution)/shard_map/ppermute | solution.py:21
  19.2 6.3 %collective-permute-start.2 = (bf16[12,6,1024]{2,1,0:T(8,128)(2,1)S(1)}, bf16[12,6,1024]{2,1,0:T(8,128)(2,1)S(1)}, u32[]{:S(2)}, u32[]{:S(2)}) collective-permute-start(bf16[12,6,1024]{2,1,0:T(8,128)(2,1)S(1)} %get-tuple-element.13), channel_id=1, source_target_pairs={{0,1},{1,2},{2,3},{3,4},{4,5},{5,6},{6,7},{7,0},{8,9},{9,10},{10,1... | collective-permute-start | bytes 442376 | tf_op jit(solution)/shard_map/ppermute | solution.py:20
  19.3 6.3 %collective-permute-start.3 = (bf16[12,6,1024]{2,1,0:T(8,128)(2,1)S(1)}, bf16[12,6,1024]{2,1,0:T(8,128)(2,1)S(1)}, u32[]{:S(2)}, u32[]{:S(2)}) collective-permute-start(bf16[12,6,1024]{2,1,0:T(8,128)(2,1)S(1)} %get-tuple-element.14), channel_id=1, source_target_pairs={{1,0},{2,1},{3,2},{4,3},{5,4},{6,5},{7,6},{0,7},{9,8},{10,9},{11,1... | collective-permute-start | bytes 442376 | tf_op jit(solution)/shard_map/ppermute | solution.py:21
  27.9 4.5 copy-start.4
  38.0 3.2 copy-start.2
  69.5 1.8 copy-start.3
  82.5 4.2 copy-start.8
  82.5 4.2 copy-start.9
  82.5 4.3 copy-start.10
  85.9 82.6 %all-gather.7.cloned.1.call-start = ((), (), s32[]{:S(2)}) async-start(), calls=%async_computation.2 | async-start | bytes 4177920 | tf_op jit(solution)/shard_map/all_gather | solution.py:133
  86.6 135.5 %reduce-scatter.4.cloned.1.call-start = ((), (), s32[]{:S(2)}) async-start(), calls=%async_computation.4 | async-start | bytes 2654208
  87.1 81.5 %copy-start.6 = (f32[5,1024]{1,0:T(8,128)S(1)}, f32[5,1024]{1,0:T(8,128)}, u32[]{:S(2)}) copy-start(f32[5,1024]{1,0:T(8,128)} %param.15) | copy-start | bytes 61444
  87.1 81.5 %copy-start.7 = (f32[5,1024]{1,0:T(8,128)S(1)}, f32[5,1024]{1,0:T(8,128)}, u32[]{:S(2)}) copy-start(f32[5,1024]{1,0:T(8,128)} %param.16) | copy-start | bytes 61444
  168.5 10.6 %copy-start.5 = (bf16[5,1024,320]{2,1,0:T(8,128)(2,1)S(1)}, bf16[5,1024,320]{2,1,0:T(8,128)(2,1)}, u32[]{:S(2)}) copy-start(bf16[5,1024,320]{2,1,0:T(8,128)(2,1)} %all-gather.7.cloned.1.call-done) | copy-start | bytes 9830404
  179.2 7.2 %copy-start.11 = (bf16[5,6,192,320]{3,2,1,0:T(8,128)(2,1)}, bf16[5,6,192,320]{3,2,1,0:T(8,128)(2,1)S(1)}, u32[]{:S(2)}) copy-start(bf16[5,6,192,320]{3,2,1,0:T(8,128)(2,1)S(1)} %multiply_convert_fusion) | copy-start | bytes 11059204
  188.1 328.3 %all-gather.9.cloned.1.call-start = ((), (), s32[]{:S(2)}) async-start(), calls=%async_computation.3 | async-start | bytes 55705600 | tf_op jit(solution)/shard_map/all_gather | solution.py:150
  562.7 28.0 %copy-start.1 = (bf16[1024,1024]{1,0:T(8,128)(2,1)S(1)}, bf16[1024,1024]{1,0:T(8,128)(2,1)}, u32[]{:S(2)}) copy-start(bf16[1024,1024]{1,0:T(8,128)(2,1)} %param.14) | copy-start | bytes 6291460
Sparse Core Ops, SparseCore 0:
  86.0 29.4 all-gather.4
  117.7 50.7 all-gather.6
  188.2 33.8 reduce-scatter.3
  224.2 292.1 all-gather.8
